TPU v7x, 128 devices: a whole 4x4x4 slice. The times are simulated.
128 devices in a mesh: scen: 8 (over y, core), vox: 16 (over x, z).
Axes of the slice: x: 4, y: 4, z: 4, core: 2. Of those that a mesh axis runs over, the one named last changes fastest.
Arguments:
- dose_blocks: float32 [16, 1280, 128, 128], P('scen', 'vox'), may hold values from 0 to 0.046875
- block_map: int32 [1280, 2], P('vox'), may hold values from 0 to 127, as said below
- block_counts: int32 [16], P('vox'), may hold values from 10 to 80, as said below
- target: float32 [262144], P('vox'), may hold values from 0.5 to 15
- fluence_init: float32 [16384], P('vox'), may hold values from 0.5 to 1.5
Outputs:
- fluence: float32 [16384], P('vox')
- weights: float32 [16, 262144], P('scen', 'vox')
Inputs may be any that keep to these rules, and one draw needn't show every extreme that they name: `block_map`: column 0 is a row block of the slot's voxel group, 0 to 127; column 1 a beamlet block, 0 to 127; pairs may repeat. `block_counts`: the slots in use are the first ones of their group; some group uses all 80.
All inputs are finite; a program needn't handle non-finite values.
Results may differ from a plain program's by a relative error of at most 0.0003.
Values sent between devices are 32-bit elements; how exact they have to be, the bound alone decides.
A program may use at most 64 MiB of HBM per device.

v0:
```python
import jax
import jax.numpy as jnp
from jax import lax
from jax.sharding import PartitionSpec as P

ROUNDS = 2
ITERS = 2


HIGHEST = lax.Precision.HIGHEST
SHARPNESS = 2.0
STEP_SIZE = 0.5


def tables(block_map, block_counts, row_blocks, beam_blocks):
    slots = jnp.arange(block_map.shape[0])
    usable = (slots < block_counts[0]).astype(jnp.float32)
    row_hot = (block_map[:, 0][:, None] == jnp.arange(row_blocks)[None, :]).astype(
        jnp.float32
    ) * usable[:, None]
    col_hot = (block_map[:, 1][:, None] == jnp.arange(beam_blocks)[None, :]).astype(jnp.float32)
    return (row_hot, col_hot)


def forward(blocks, row_hot, col_hot, copies):
    scen_here = copies.shape[0]
    side = blocks.shape[2]
    pieces = copies.reshape(scen_here, col_hot.shape[1], side)
    picked = jnp.einsum("nb,sbj->snj", col_hot, pieces, precision=HIGHEST)
    products = jnp.einsum("snij,snj->sni", blocks, picked, precision=HIGHEST)
    summed = jnp.einsum("nr,sni->sri", row_hot, products, precision=HIGHEST)
    return summed.reshape(scen_here, row_hot.shape[1] * side)


def backward(blocks, row_hot, col_hot, weighted):
    scen_here = weighted.shape[0]
    side = blocks.shape[2]
    pieces = weighted.reshape(scen_here, row_hot.shape[1], side)
    picked = jnp.einsum("nr,sri->sni", row_hot, pieces, precision=HIGHEST)
    products = jnp.einsum("snij,sni->snj", blocks, picked, precision=HIGHEST)
    summed = jnp.einsum("nb,snj->sbj", col_hot, products, precision=HIGHEST)
    return summed.reshape(scen_here, col_hot.shape[1] * side)


def scenario_weights(score):
    peak = lax.pmax(jnp.max(score, axis=0), "scen")
    total = lax.psum(jnp.sum(jnp.exp(score - peak[None, :]), axis=0), "scen")
    return jnp.exp(score - peak[None, :]) / total[None, :]


def body(dose_blocks, block_map, block_counts, target, fluence_init):
    side = dose_blocks.shape[2]
    scen_here = dose_blocks.shape[0]
    share = fluence_init.shape[0]
    beamlets = share * lax.axis_size("vox")
    row_hot, col_hot = tables(block_map, block_counts, target.shape[0] // side, beamlets // side)
    scen_total = scen_here * lax.axis_size("scen")
    weights = jnp.zeros((scen_here, target.shape[0]), jnp.float32)
    fluence = fluence_init
    for outer_round in range(ROUNDS):
        copies = jnp.broadcast_to(fluence[None, :], (scen_here, share))
        for inner_step in range(ITERS):
            whole = lax.all_gather(copies, "vox", axis=1, tiled=True)
            dose = forward(dose_blocks, row_hot, col_hot, whole)
            excess = dose - target[None, :]
            if inner_step == 0:
                weights = scenario_weights(SHARPNESS * excess * excess)
            terms = backward(dose_blocks, row_hot, col_hot, 2.0 * weights * excess)
            gradient = lax.psum_scatter(terms, "vox", scatter_dimension=1, tiled=True)
            copies = jnp.maximum(copies - STEP_SIZE * gradient, 0.0)
        fluence = lax.psum(jnp.sum(copies, axis=0), "scen") / scen_total
    return (fluence, weights)


def solution(mesh):
    placed = (P("scen", "vox", None, None), P("vox", None), P("vox"), P("vox"), P("vox"))
    return jax.shard_map(
        body, mesh=mesh, in_specs=placed, out_specs=(P("vox"), P("scen", "vox")), check_vma=False
    )
```

profile of v0, /device:TPU:1, one launch (start us, length us, event | category | flops | bytes accessed | tf_op | source)
XLA Modules:
  0.0 893.7 jit_solution(14443355712869102597)
XLA Ops:
  7.9 0.8 slice_bitcast_fusion
  8.6 0.9 copy.27
  9.6 20.5 %all_gather.16 = f32[16384]{0:T(1024)S(1)} all-gather(f32[1024]{0:T(1024)} %param.9), channel_id=2, replica_groups=mesh['scen'=8,'vox'=16] {'vox'}, dimensions={0}, use_global_device_ids=true | all-gather | bytes 69632 | tf_op jit(solution)/shard_map/all_gather | solution.py:63
  30.4 18.9 %fusion.105 = f32[2,80,1,128]{3,2,1,0:T(1,128)S(1)} fusion(f32[2,80,128,1]{2,3,1,0:T(1,128)S(1)} %bitcast.202, f32[2,80,128,128]{3,2,1,0:T(8,128)} %param.5), kind=kOutput, calls=%fused_computation.126 | convolution fusion | flops 31457280 | bytes 10649600 | tf_op jit(solution)/shard_map/snij,snj->sni/dot_general | solution.py:30
  49.3 1.1 fusion.27
  50.4 62.2 %all-reduce.5.cloned.1.call-done = f32[128,128]{0,1:T(8,128)} async-done(((f32[128,128]{0,1:T(8,128)}), f32[128,128]{0,1:T(8,128)}) %all-reduce.5.cloned.1.call-update) | async-done | bytes 65552 | tf_op jit(solution)/shard_map/pmax | solution.py:46
  112.6 1.5 fusion.25
  114.4 59.9 %all-reduce.7.cloned.1.call-done = f32[128,128]{0,1:T(8,128)} async-done(((f32[128,128]{0,1:T(8,128)}), f32[128,128]{0,1:T(8,128)}) %all-reduce.7.cloned.1.call-update) | async-done | bytes 65552 | tf_op jit(solution)/shard_map/psum | solution.py:47
  174.3 1.2 fusion.22
  175.5 11.4 %fusion.106 = f32[2,80,1,128]{3,2,1,0:T(1,128)S(1)} fusion(f32[2,80,128,1]{2,3,1,0:T(1,128)S(1)} %bitcast.219, f32[2,80,128,128]{3,2,1,0:T(8,128)} %param.5), kind=kOutput, calls=%fused_computation.127 | convolution fusion | flops 31457280 | bytes 10649600 | tf_op jit(solution)/shard_map/snij,sni->snj/dot_general | solution.py:40
  186.9 0.3 convolution_bitcast_fusion.3
  187.2 7.5 copy.69
  194.8 86.0 %reduce-scatter.13.cloned.1.call-done = f32[1024,2]{1,0:T(8,128)} async-done(((f32[16384,2]{1,0:T(8,128)}), f32[1024,2]{1,0:T(8,128)}) %reduce-scatter.13.cloned.1.call-update) | async-done | bytes 8208
  280.8 1.2 copy.62
  282.1 17.9 %all_gather.13 = f32[2,16384]{1,0:T(2,128)S(1)} all-gather(f32[2,1024]{1,0:T(2,128)S(1)} %subtract_maximum_fusion.1), channel_id=1, replica_groups=mesh['scen'=8,'vox'=16] {'vox'}, dimensions={1}, use_global_device_ids=true | all-gather | bytes 139264 | tf_op jit(solution)/shard_map/all_gather | solution.py:63
  300.2 18.9 %fusion.107 = f32[2,80,1,128]{3,2,1,0:T(1,128)S(1)} fusion(f32[2,80,128,1]{2,3,1,0:T(1,128)S(1)} %bitcast.204, f32[2,80,128,128]{3,2,1,0:T(8,128)} %param.5), kind=kOutput, calls=%fused_computation.128 | convolution fusion | flops 31457280 | bytes 10649600 | tf_op jit(solution)/shard_map/snij,snj->sni/dot_general | solution.py:30
  319.1 0.4 fusion.2
  319.9 11.4 %fusion.108 = f32[2,80,1,128]{3,2,1,0:T(1,128)S(1)} fusion(f32[2,80,128,1]{2,3,1,0:T(1,128)S(1)} %bitcast.205, f32[2,80,128,128]{3,2,1,0:T(8,128)} %param.5), kind=kOutput, calls=%fused_computation.129 | convolution fusion | flops 31457280 | bytes 10649600 | tf_op jit(solution)/shard_map/snij,sni->snj/dot_general | solution.py:40
  331.3 0.3 convolution_bitcast_fusion.2
  331.7 18.7 %copy.70 = f32[2,128,128]{0,2,1:T(8,128)} copy(f32[2,128,128]{1,2,0:T(8,128)S(1)} %convolution_bitcast_fusion.2) | data formatting | bytes 262144
  350.4 90.3 %reduce-scatter.15.cloned.1.call-done = f32[1024,2]{1,0:T(8,128)} async-done(((f32[16384,2]{1,0:T(8,128)}), f32[1024,2]{1,0:T(8,128)}) %reduce-scatter.15.cloned.1.call-update) | async-done | bytes 8208
  440.7 1.2 copy.64
  442.0 14.0 %psum.29 = f32[1024]{0:T(1024)S(1)} all-reduce(f32[1024]{0:T(1024)S(1)} %maximum_reduce_fusion.1), channel_id=1, replica_groups=mesh['scen'=8,'vox'=16] {'scen'}, use_global_device_ids=true, to_apply=%region_7.0 | all-reduce | flops 1024 | bytes 8192 | tf_op jit(solution)/shard_map/psum | solution.py:71
  456.0 17.6 %all_gather.17 = f32[16384]{0:T(1024)S(1)} all-gather(f32[1024]{0:T(1024)S(1)} %broadcast_multiply_fusion.1), channel_id=3, replica_groups=mesh['scen'=8,'vox'=16] {'vox'}, dimensions={0}, use_global_device_ids=true | all-gather | bytes 69632 | tf_op jit(solution)/shard_map/all_gather | solution.py:63
  473.9 18.9 %fusion.109 = f32[2,80,1,128]{3,2,1,0:T(1,128)S(1)} fusion(f32[2,80,128,1]{2,3,1,0:T(1,128)S(1)} %bitcast.207, f32[2,80,128,128]{3,2,1,0:T(8,128)} %param.5), kind=kOutput, calls=%fused_computation.130 | convolution fusion | flops 31457280 | bytes 10649600 | tf_op jit(solution)/shard_map/snij,snj->sni/dot_general | solution.py:30
  492.8 0.4 fusion.28
  493.3 0.7 copy.32
  494.1 59.6 %all-reduce.9.cloned.1.call-done = f32[16384]{0:T(1024)} async-done(((f32[16384]{0:T(1024)}), f32[16384]{0:T(1024)}) %all-reduce.9.cloned.1.call-update) | async-done | bytes 65552 | tf_op jit(solution)/shard_map/pmax | solution.py:46
  553.7 0.9 copy.33
  554.7 0.7 copy.34
  555.5 59.7 %all-reduce.11.cloned.1.call-done = f32[16384]{0:T(1024)} async-done(((f32[16384]{0:T(1024)}), f32[16384]{0:T(1024)}) %all-reduce.11.cloned.1.call-update) | async-done | bytes 65552 | tf_op jit(solution)/shard_map/psum | solution.py:47
  615.2 0.9 copy.35
  616.1 0.3 fusion.20
  616.4 11.4 %fusion.110 = f32[2,80,1,128]{3,2,1,0:T(1,128)S(1)} fusion(f32[2,80,128,1]{2,3,1,0:T(1,128)S(1)} %bitcast.220, f32[2,80,128,128]{3,2,1,0:T(8,128)} %param.5), kind=kOutput, calls=%fused_computation.131 | convolution fusion | flops 31457280 | bytes 10649600 | tf_op jit(solution)/shard_map/snij,sni->snj/dot_general | solution.py:40
  627.9 0.3 convolution_bitcast_fusion.1
  628.2 7.5 copy.71
  635.9 86.0 %reduce-scatter.17.cloned.1.call-done = f32[1024,2]{1,0:T(8,128)} async-done(((f32[16384,2]{1,0:T(8,128)}), f32[1024,2]{1,0:T(8,128)}) %reduce-scatter.17.cloned.1.call-update) | async-done | bytes 8208
  721.9 1.2 copy.66
  723.2 17.6 %all_gather.15 = f32[2,16384]{1,0:T(2,128)S(1)} all-gather(f32[2,1024]{1,0:T(2,128)S(1)} %subtract_maximum_fusion), channel_id=1, replica_groups=mesh['scen'=8,'vox'=16] {'vox'}, dimensions={1}, use_global_device_ids=true | all-gather | bytes 139264 | tf_op jit(solution)/shard_map/all_gather | solution.py:63
  741.0 19.1 %fusion.111 = f32[2,80,1,128]{3,2,1,0:T(1,128)S(1)} fusion(f32[2,80,128,1]{2,3,1,0:T(1,128)S(1)} %bitcast.209, f32[2,80,128,128]{3,2,1,0:T(8,128)} %param.5), kind=kOutput, calls=%fused_computation.132 | convolution fusion | flops 31457280 | bytes 10649600 | tf_op jit(solution)/shard_map/snij,snj->sni/dot_general | solution.py:30
  760.1 0.4 fusion.4
  760.9 11.4 %fusion.112 = f32[2,80,1,128]{3,2,1,0:T(1,128)S(1)} fusion(f32[2,80,128,1]{2,3,1,0:T(1,128)S(1)} %bitcast.200, f32[2,80,128,128]{3,2,1,0:T(8,128)} %param.5), kind=kOutput, calls=%fused_computation.133 | convolution fusion | flops 31457280 | bytes 10649600 | tf_op jit(solution)/shard_map/snij,sni->snj/dot_general | solution.py:40
  772.7 7.5 copy.72
  780.2 0.9 fusion.7
  781.1 89.6 %reduce-scatter.19.cloned.1.call-done = f32[1024,2]{1,0:T(8,128)} async-done(((f32[16384,2]{1,0:T(8,128)}), f32[1024,2]{1,0:T(8,128)}) %reduce-scatter.19.cloned.1.call-update) | async-done | bytes 8208
  870.7 1.2 copy.68
  871.9 14.0 %psum.31 = f32[1024]{0:T(1024)S(1)} all-reduce(f32[1024]{0:T(1024)S(1)} %maximum_reduce_fusion), channel_id=1, replica_groups=mesh['scen'=8,'vox'=16] {'scen'}, use_global_device_ids=true, to_apply=%region_15.0 | all-reduce | flops 1024 | bytes 8192 | tf_op jit(solution)/shard_map/psum | solution.py:71
  885.9 0.6 broadcast_multiply_fusion
  (45 shorter events, 2.9 us)
Async XLA Ops:
  7.2 105.5 %all-reduce.5.cloned.1.call-start = ((), (), s32[]{:S(2)}) async-start(), calls=%async_computation.4 | async-start | bytes 131072 | tf_op jit(solution)/shard_map/pmax | solution.py:46
  50.4 123.9 %all-reduce.7.cloned.1.call-start = ((), (), s32[]{:S(2)}) async-start(), calls=%async_computation.5 | async-start | bytes 131072 | tf_op jit(solution)/shard_map/psum | solution.py:47
  114.2 166.7 %reduce-scatter.13.cloned.1.call-start = ((), (), s32[]{:S(2)}) async-start(), calls=%async_computation.8 | async-start | bytes 8912896
  186.9 95.1 %copy-start.4 = (f32[1024]{0:T(1024)S(1)}, f32[1024]{0:T(1024)}, u32[]{:S(2)}) copy-start(f32[1024]{0:T(1024)} %param.9) | copy-start | bytes 12292
  194.8 124.4 %copy-start.3 = (f32[128,128]{0,1:T(8,128)S(1)}, f32[128,128]{0,1:T(8,128)}, u32[]{:S(2)}) copy-start(f32[128,128]{0,1:T(8,128)} %all-reduce.5.cloned.1.call-done) | copy-start | bytes 196612
  194.8 124.4 %copy-start.5 = (f32[128,128]{0,1:T(8,128)S(1)}, f32[128,128]{0,1:T(8,128)}, u32[]{:S(2)}) copy-start(f32[128,128]{0,1:T(8,128)} %all-reduce.7.cloned.1.call-done) | copy-start | bytes 196612
  194.8 245.9 %reduce-scatter.15.cloned.1.call-start = ((), (), s32[]{:S(2)}) async-start(), calls=%async_computation.9 | async-start | bytes 8912896
  350.4 203.3 %all-reduce.9.cloned.1.call-start = ((), (), s32[]{:S(2)}) async-start(), calls=%async_computation.6 | async-start | bytes 131072 | tf_op jit(solution)/shard_map/pmax | solution.py:46
  494.0 121.2 %all-reduce.11.cloned.1.call-start = ((), (), s32[]{:S(2)}) async-start(), calls=%async_computation.7 | async-start | bytes 131072 | tf_op jit(solution)/shard_map/psum | solution.py:47
  555.4 166.5 %reduce-scatter.17.cloned.1.call-start = ((), (), s32[]{:S(2)}) async-start(), calls=%async_computation.10 | async-start | bytes 8912896
  635.8 234.9 %reduce-scatter.19.cloned.1.call-start = ((), (), s32[]{:S(2)}) async-start(), calls=%async_computation.11 | async-start | bytes 8912896
  772.3 7.9 copy-start
  772.3 7.9 copy-start.1
  772.3 7.9 copy-start.2
Sparse Core Ops, SparseCore 0:
  50.5 62.0 all-reduce.4
  115.5 58.7 all-reduce.6
  194.9 85.8 reduce-scatter.12
  350.5 90.2 reduce-scatter.14
  494.1 59.4 all-reduce.8
  556.4 58.7 all-reduce.10
  635.9 86.0 reduce-scatter.16
  780.3 90.2 reduce-scatter.18
where the time goes:
time: 900 us; the launch traced here: 894 us
  waiting for transfers between devices  593 us (66%)
  matrix products  128 us (14%)
  blocking collectives  101 us (11%)
  local copies, waits for them, and re-layouts  51.3 us (6%)
  between operations  15.4 us (2%)
    unnamed x12, waiting for transfers between devices  352 us
    pmax x2, waiting for transfers between devices, scenario_weights(): peak = lax.pmax(jnp.max(score, axis=0), 'scen')  122 us
    psum x2, waiting for transfers between devices, scenario_weights(): total = lax.psum(jnp.sum(jnp.exp(score - peak[None, :]), axis=0), 'scen')  120 us
    dot_general x4, matrix products, forward(): products = jnp.einsum('snij,snj->sni', blocks, picked, precision=HIGHEST)  75.9 us
    all_gather x4, blocking collectives, body(): whole = lax.all_gather(copies, 'vox', axis=1, tiled=True)  73.6 us
    unnamed x22, local copies, waits for them, and re-layouts  46.2 us
    dot_general x4, matrix products, backward(): products = jnp.einsum('snij,sni->snj', blocks, picked, precision=HIGHEST)  45.8 us
    psum x2, blocking collectives, body(): fluence = lax.psum(jnp.sum(copies, axis=0), 'scen') / scen_total  27.9 us
  transfers between devices with their start and end apart: 8, of which 8 were waited for; matrix products, arithmetic and copies ran while one was open for 0% of the time, Pallas kernels for 0%

commit v1 on v0

v1 whole, which is shorter than its diff:
```python
import functools

import jax
import jax.numpy as jnp
from jax import lax
from jax.experimental import pallas as pl
from jax.experimental.pallas import tpu as pltpu
from jax.sharding import PartitionSpec as P

ROUNDS = 2
SHARPNESS = 2.0
STEP_SIZE = 0.5
F32 = jnp.float32
BF16 = jnp.bfloat16
MESH = pl.DeviceIdType.MESH
UNROLL = 20
LOADS = 8


def split3(x):
    high = x.astype(BF16)
    rest = x - high.astype(F32)
    mid = rest.astype(BF16)
    low = (rest - mid.astype(F32)).astype(BF16)
    return high, mid, low


def mm(a, b):
    return lax.dot_general(a, b, (((1,), (0,)), ((), ())), preferred_element_type=F32)


def mm_nt(a, b):
    return lax.dot_general(a, b, (((1,), (1,)), ((), ())), preferred_element_type=F32)


def iota(shape, dim):
    return lax.broadcasted_iota(jnp.int32, shape, dim)


def vox_partners(nv, v):
    if nv == 16:
        x, z = v // 4, lax.rem(v, 4)
        hops = [(dx, dz) for dx in range(4) for dz in range(4) if dx or dz]
        hops.sort(key=lambda h: -(min(h[0], 4 - h[0]) + min(h[1], 4 - h[1])))
        return [lax.rem(x + dx, 4) * 4 + lax.rem(z + dz, 4) for dx, dz in hops]
    return [lax.rem(v + k, nv) for k in range(1, nv)]


def kernel(
    nv, ns, slots,
    map_ref, count_ref, target_ref, init_ref, dose_ref,
    out_ref, weights_ref,
    stage, fwd_w, bwd_w, left, right, got_left, got_right,
    col_hot, same3, col3, rep3, spare, target_slot, excess_ref, held_w, copies,
    whole, terms, parts, sums, lse_half, lse_parts, lse_all,
    load_sem, vox_send, vox_recv, scen_send, scen_recv, lse_send, lse_recv,
):
    half = slots // 2
    beam_blocks = nv * 8
    v = lax.axis_index("vox")
    s_me = lax.axis_index("scen")
    ny = ns // 2
    y_me, core = s_me // 2, lax.rem(s_me, 2)
    own = pl.ds(pl.multiple_of(v * 8, 8), 8)
    vox_others = vox_partners(nv, v)
    scen_others = [lax.rem(s_me + k, ns) for k in range(1, ns)]
    twin = s_me + 1 - 2 * core
    chips = [lax.rem(y_me + k, ny) * 2 + core for k in range(1, ny)]
    per_load = slots // LOADS

    def load(s, k):
        rows = pl.ds(k * per_load, per_load)
        return pltpu.make_async_copy(
            dose_ref.at[s, rows], stage.at[s, rows], load_sem.at[s, k]
        )

    for s in range(2):
        for k in range(LOADS):
            load(s, k).start()

    barrier = pltpu.get_barrier_semaphore()
    for t in vox_others:
        pl.semaphore_signal(barrier, inc=1, device_id={"vox": t}, device_id_type=MESH)
    for t in scen_others:
        pl.semaphore_signal(barrier, inc=1, device_id={"scen": t}, device_id_type=MESH)

    left[...] = jnp.zeros_like(left)
    right[...] = jnp.zeros_like(right)

    usable = (iota((slots, 128), 0) < count_ref[0]).astype(F32)
    row_hot = (map_ref[:, 0:1] == iota((slots, 128), 1)).astype(F32) * usable
    col_of = (map_ref[:, 1:2] == iota((slots, beam_blocks), 1)).astype(F32)
    eye_row = (iota((128, 128), 0) == iota((128, 128), 1)).astype(BF16)
    eye_col = (iota((beam_blocks, beam_blocks), 0) == iota((beam_blocks, beam_blocks), 1)).astype(BF16)
    row_b, col_b = row_hot.astype(BF16), col_of.astype(BF16)
    col_hot[...] = col_b
    same3[...] = mm_nt(row_b, jnp.concatenate([row_b] * 3, axis=0)).astype(BF16)
    col3[...] = mm_nt(eye_col, jnp.concatenate([col_b] * 3, axis=0)).astype(BF16)
    same = mm_nt(row_b, row_b)
    earlier = jnp.sum(
        jnp.where(iota((slots, slots), 1) < iota((slots, slots), 0), same, 0.0),
        axis=1, keepdims=True,
    )
    rep_b = jnp.where(earlier < 0.5, row_hot, 0.0).astype(BF16)
    picks = mm_nt(eye_row, jnp.concatenate([rep_b] * 3, axis=0))
    rep3[...] = picks.astype(BF16)
    covered = jnp.sum(picks, axis=1, keepdims=True)
    spare[...] = jnp.broadcast_to(jnp.where(covered > 0.5, 0.0, 1.0 / (2 * ns)), (128, 128))
    tgt = mm(row_b, jnp.concatenate(split3(target_ref[...]), axis=1))
    target_slot[...] = (tgt[:, 0:128] + tgt[:, 128:256]) + tgt[:, 256:384]

    pl.semaphore_wait(barrier, len(vox_others) + len(scen_others))

    def vox_copy(src, dst, slot, target):
        return pltpu.make_async_remote_copy(
            src_ref=src, dst_ref=dst, send_sem=vox_send.at[slot], recv_sem=vox_recv.at[slot],
            device_id={"vox": target}, device_id_type=MESH,
        )

    def vox_wait(slot, ref):
        rest = ref.at[pl.ds(0, (nv - 1) * 8)]
        pltpu.make_async_copy(rest, rest, vox_recv.at[slot]).wait()

    def gather_slot(r, s):
        return 2 + 2 * r + s

    def reduce_slot(r, step, s):
        return 6 + 4 * r + 2 * step + s

    whole[0, own, :] = init_ref[...]
    for t in vox_others:
        vox_copy(init_ref, whole.at[0, own], 0, t).start()

    def send_whole(slot, value):
        whole[slot, own, :] = value
        for t in vox_others:
            vox_copy(whole.at[slot, own], whole.at[slot, own], slot, t).start()

    def convert(s, k):
        load(s, k).wait()
        for u in range(per_load):
            n = k * per_load + u
            pair = lax.rem(n, half)
            at = pl.ds(pl.multiple_of((n // half) * 128, 128), 128)
            block = stage[s, n]
            high = block.astype(BF16)
            low = (block - high.astype(F32)).astype(BF16)
            bwd_w[s, pair, at, 0:128] = high
            bwd_w[s, pair, at, 128:256] = low
            fwd_w[s, pair, at, 0:128] = high.T
            fwd_w[s, pair, at, 128:256] = low.T

    for s in range(2):
        lax.fori_loop(0, LOADS, lambda k, c: (convert(s, k), c)[1], 0)

    def stack(s, pieces):
        for q, piece in enumerate(pieces):
            left[s, pl.ds(q, half, stride=8), :] = piece[0:half]
            right[s, pl.ds(q + 3, half, stride=8), :] = piece[half:slots]

    def multiply(s, weights):
        def some(g, carry):
            for u in range(UNROLL):
                p = g * UNROLL + u
                at = pl.ds(pl.multiple_of(p * 8, 8), 8)
                lhs = jnp.concatenate([left[s, at, :], right[s, at, :]], axis=1).astype(BF16)
                got = mm(lhs, weights[s, p])
                got_left[s, at, :] = got[:, 0:128]
                got_right[s, at, :] = got[:, 128:256]
            return carry

        lax.fori_loop(0, half // UNROLL, some, 0)
        halves = []
        for base in (0, 3):
            total = None
            for q in (2, 1, 0):
                at = pl.ds(base + q, half, stride=8)
                term = got_left[s, at, :] + got_right[s, at, :]
                total = term if total is None else total + term
            halves.append(total)
        return jnp.concatenate(split3(jnp.concatenate(halves, axis=0)), axis=0)

    def pick(slot):
        picked = mm(col_hot[...], jnp.concatenate(split3(whole[slot]), axis=1))
        return [picked[:, 128 * q:128 * q + 128] for q in range(3)]

    def forward(s, pieces):
        stack(s, pieces)
        return mm(same3[...], multiply(s, fwd_w)) - target_slot[...]

    def backward(r, step, s, weighted):
        slot = reduce_slot(r, step, s)
        k = slot - 6
        stack(s, [piece.astype(F32) for piece in split3(weighted)])
        terms[k] = mm(col3[...], multiply(s, bwd_w))
        for t in vox_others:
            vox_copy(
                terms.at[k, pl.ds(pl.multiple_of(t * 8, 8), 8)],
                parts.at[k, own], slot, t,
            ).start()
        parts[k, own, :] = terms[k, own, :]

    def descend(r, step, s):
        slot = reduce_slot(r, step, s)
        k = slot - 6
        vox_wait(slot, parts.at[k])
        gradient = parts[k, 0:8, :]
        for j in range(1, nv):
            gradient = gradient + parts[k, 8 * j:8 * j + 8, :]
        moved = jnp.maximum(copies[s] - STEP_SIZE * gradient, 0.0)
        copies[s] = moved
        return moved

    def merge(values):
        peak = functools.reduce(jnp.maximum, values)
        return peak + jnp.log(sum(jnp.exp(value - peak) for value in values))

    mine = pl.ds(pl.multiple_of(core * half, 8), half)
    other = pl.ds(pl.multiple_of((1 - core) * half, 8), half)

    def lse_copy(src, dst, r, k, target):
        return pltpu.make_async_remote_copy(
            src_ref=src, dst_ref=dst, send_sem=lse_send.at[r, k], recv_sem=lse_recv.at[r, k],
            device_id={"scen": target}, device_id_type=MESH,
        )

    def log_totals(r, scores):
        lse_all[2 * r] = merge(scores)
        first = lse_copy(lse_all.at[2 * r, other], lse_half.at[r], r, 0, twin)
        first.start()
        first.wait_recv()
        chip = merge([lse_all[2 * r, mine, :], lse_half[r]])
        spot = pl.ds(pl.multiple_of(y_me * half, 8), half)
        lse_parts[r, spot, :] = chip
        for t in chips:
            lse_copy(lse_parts.at[r, spot], lse_parts.at[r, spot], r, 1, t).start()
        rest = lse_parts.at[r, pl.ds(0, (ny - 1) * half)]
        pltpu.make_async_copy(rest, rest, lse_recv.at[r, 1]).wait()
        lse_all[2 * r + 1, mine, :] = merge(
            [lse_parts[r, half * j:half * j + half, :] for j in range(ny)]
        )
        last = lse_copy(
            lse_all.at[2 * r + 1, mine], lse_all.at[2 * r + 1, mine], r, 2, twin
        )
        last.start()
        last.wait_recv()
        return lse_all[2 * r + 1]

    def scen_copy(r, t):
        return pltpu.make_async_remote_copy(
            src_ref=sums.at[r, s_me], dst_ref=sums.at[r, s_me],
            send_sem=scen_send.at[r], recv_sem=scen_recv.at[r],
            device_id={"scen": t}, device_id_type=MESH,
        )

    for s in range(2):
        copies[s] = init_ref[...]

    for r in range(ROUNDS):
        vox_wait(r, whole.at[r])
        pieces = pick(r)
        scores = []
        for s in range(2):
            excess = forward(s, pieces)
            excess_ref[s] = excess
            scores.append(SHARPNESS * excess * excess)
        totals = log_totals(r, scores)
        for s in range(2):
            excess = excess_ref[s]
            held = jnp.exp(SHARPNESS * excess * excess - totals)
            held_w[s] = held
            backward(r, 0, s, 2.0 * held * excess)
        if r == ROUNDS - 1:
            for s in range(2):
                pieces = jnp.concatenate(split3(held_w[s]), axis=0)
                weights_ref[s] = mm(rep3[...], pieces) + spare[...]
        for s in range(2):
            send_whole(gather_slot(r, s), descend(r, 0, s))
        for s in range(2):
            slot = gather_slot(r, s)
            vox_wait(slot, whole.at[slot])
            excess = forward(s, pick(slot))
            backward(r, 1, s, 2.0 * held_w[s] * excess)
        moved = descend(r, 1, 0)
        sums[r, s_me] = moved + descend(r, 1, 1)
        for t in scen_others:
            scen_copy(r, t).start()
        pltpu.make_async_copy(
            sums.at[r, pl.ds(0, ns - 1)], sums.at[r, pl.ds(0, ns - 1)], scen_recv.at[r]
        ).wait()
        total = sums[r, 0]
        for j in range(1, ns):
            total = total + sums[r, j]
        fluence = total / (2 * ns)
        if r < ROUNDS - 1:
            for s in range(2):
                copies[s] = fluence
            send_whole(r + 1, fluence)
        else:
            out_ref[...] = fluence

    for slot in range(6 + 4 * ROUNDS):
        rest = whole.at[0, pl.ds(0, (nv - 1) * 8)]
        pltpu.make_async_copy(rest, rest, vox_send.at[slot]).wait()
    for r in range(ROUNDS):
        rest = sums.at[r, pl.ds(0, ns - 1)]
        pltpu.make_async_copy(rest, rest, scen_send.at[r]).wait()
        for k, part in ((0, lse_half.at[r]), (1, lse_parts.at[r, pl.ds(0, (ny - 1) * half)]), (2, lse_half.at[r])):
            pltpu.make_async_copy(part, part, lse_send.at[r, k]).wait()


def body(nv, ns, dose_blocks, block_map, block_counts, target, fluence_init):
    _, slots, side, _ = dose_blocks.shape
    half = slots // 2
    rows = target.shape[0] // side
    beam_blocks = nv * 8
    vmem = pl.BlockSpec(memory_space=pltpu.VMEM)
    out, weights = pl.pallas_call(
        functools.partial(kernel, nv, ns, slots),
        out_shape=(
            jax.ShapeDtypeStruct((8, side), F32),
            jax.ShapeDtypeStruct((2, rows, side), F32),
        ),
        in_specs=[vmem, pl.BlockSpec(memory_space=pltpu.SMEM), vmem, vmem, pl.BlockSpec(memory_space=pl.ANY)],
        out_specs=(vmem, vmem),
        scratch_shapes=[
            pltpu.VMEM((2, slots, side, side), F32),
            pltpu.VMEM((2, half, 2 * side, 2 * side), BF16),
            pltpu.VMEM((2, half, 2 * side, 2 * side), BF16),
            pltpu.VMEM((2, 8 * half, side), F32),
            pltpu.VMEM((2, 8 * half, side), F32),
            pltpu.VMEM((2, 8 * half, side), F32),
            pltpu.VMEM((2, 8 * half, side), F32),
            pltpu.VMEM((slots, beam_blocks), BF16),
            pltpu.VMEM((slots, 3 * slots), BF16),
            pltpu.VMEM((beam_blocks, 3 * slots), BF16),
            pltpu.VMEM((rows, 3 * slots), BF16),
            pltpu.VMEM((rows, side), F32),
            pltpu.VMEM((slots, side), F32),
            pltpu.VMEM((2, slots, side), F32),
            pltpu.VMEM((2, slots, side), F32),
            pltpu.VMEM((2, 8, side), F32),
            pltpu.VMEM((6, beam_blocks, side), F32),
            pltpu.VMEM((8, beam_blocks, side), F32),
            pltpu.VMEM((8, beam_blocks, side), F32),
            pltpu.VMEM((ROUNDS, ns, 8, side), F32),
            pltpu.VMEM((ROUNDS, half, side), F32),
            pltpu.VMEM((ROUNDS, ns // 2 * half, side), F32),
            pltpu.VMEM((2 * ROUNDS, slots, side), F32),
            pltpu.SemaphoreType.DMA((2, LOADS)),
            pltpu.SemaphoreType.DMA((14,)),
            pltpu.SemaphoreType.DMA((14,)),
            pltpu.SemaphoreType.DMA((ROUNDS,)),
            pltpu.SemaphoreType.DMA((ROUNDS,)),
            pltpu.SemaphoreType.DMA((ROUNDS, 3)),
            pltpu.SemaphoreType.DMA((ROUNDS, 3)),
        ],
        compiler_params=pltpu.CompilerParams(
            collective_id=0, has_side_effects=True, vmem_limit_bytes=56 * 2**20
        ),
        name="robust_descent",
    )(
        block_map, block_counts, target.reshape(rows, side), fluence_init.reshape(8, side), dose_blocks
    )
    return out.reshape(-1), weights.reshape(2, -1)


def solution(mesh):
    nv, ns = mesh.shape["vox"], mesh.shape["scen"]
    placed = (P("scen", "vox", None, None), P("vox", None), P("vox"), P("vox"), P("vox"))
    return jax.shard_map(
        functools.partial(body, nv, ns),
        mesh=mesh, in_specs=placed, out_specs=(P("vox"), P("scen", "vox")), check_vma=False,
    )
```

time: 900 us -> 86.7 us (0.10)
  waiting for transfers between devices: 593 us -> 0 us
  matrix products: 128 us -> 0 us
  blocking collectives: 101 us -> 0 us
  Pallas kernels: 0 us -> 80.9 us
  local copies, waits for them, and re-layouts: 51.3 us -> 4.33 us
  between operations: 15.4 us -> 1.29 us
    unnamed x12 -> x0, waiting for transfers between devices: 352 us -> none
    dot_general x24 -> x0, matrix products: 128 us -> none  [the longest x4 75.9 us: forward(): products = jnp.einsum('snij,snj->sni', blocks, picked, precision=HIGHEST)]
    pmax x2 -> x0, waiting for transfers between devices: 122 us -> none  [scenario_weights(): peak = lax.pmax(jnp.max(score, axis=0), 'scen')]
    psum x2 -> x0, waiting for transfers between devices: 120 us -> none  [scenario_weights(): total = lax.psum(jnp.sum(jnp.exp(score - peak[None, :]), axis=0), 'scen')]
    pallas_call x0 -> x1, Pallas kernels: none -> 80.9 us  [body(): pl.pallas_call(functools.partial(kernel, nv, ns, slots), out_shape=(jax.S...]
    all_gather x4 -> x0, blocking collectives: 73.6 us -> none  [body(): whole = lax.all_gather(copies, 'vox', axis=1, tiled=True)]
    unnamed x22 -> x3, local copies, waits for them, and re-layouts: 46.2 us -> 4.33 us
    psum x2 -> x0, blocking collectives: 27.9 us -> none  [body(): fluence = lax.psum(jnp.sum(copies, axis=0), 'scen') / scen_total]
  transfers between devices with their start and end apart: 8 -> 0, of which waited for: 8 -> 0; matrix products, arithmetic and copies ran while one was open for 0% -> 0% of each run, Pallas kernels for 0% -> 0%
where the time goes in v1:
time: 86.7 us; the launch traced here: 86.5 us
  Pallas kernels  80.9 us (93%)
  local copies, waits for them, and re-layouts  4.33 us (5%)
  between operations  1.29 us (1%)
    pallas_call x1, Pallas kernels, body(): pl.pallas_call(functools.partial(kernel, nv, ns, slots), out_shape=(jax.S...  80.9 us
    unnamed x3, local copies, waits for them, and re-layouts  4.33 us

profile of v1, /device:TPU:1, one launch (start us, length us, event | category | flops | bytes accessed | tf_op | source)
XLA Modules:
  0.0 86.5 jit_solution(12052444465965351432)
XLA Ops:
  1.3 1.4 %copy.7.map_ref = s32[80,2]{1,0:T(8,128)} copy(s32[80,2]{0,1:T(2,128)} %param.6) | data formatting | bytes 1280 | tf_op args[1]
  2.7 80.9 %robust_descent.1 = (f32[8,128]{1,0:T(8,128)}, f32[2,128,128]{2,1,0:T(8,128)}) custom-call(s32[80,2]{1,0:T(8,128)} %copy.7.map_ref, s32[1]{0:T(128)S(6)} %copy.12.count_ref, f32[128,128]{1,0:T(8,128)} %bitcast.9, f32[8,128]{1,0:T(8,128)} %bitcast.10, f32[2,80,128,128]{3,2,1,0:T(8,128)} %dose_ref.1), custom_call_target="tpu_custom_call" | custom-call | tf_op jit(solution)/shard_map/robust_descent/pallas_call | solution.py:318
  83.6 1.7 %copy.10 = f32[1,2,128,128]{3,1,2,0:T(2,128)} copy(f32[1,2,128,128]{3,2,1,0:T(8,128)} %bitcast.8) | data formatting | bytes 262144
  85.2 1.3 %copy.13 = f32[1024]{0:T(1024)} copy(f32[1024]{0:T(1024)} %bitcast.11) | data formatting | bytes 8192

commit v2 on v1

v2 whole, which is shorter than its diff:
```python
import functools

import jax
import jax.numpy as jnp
from jax import lax
from jax.experimental import pallas as pl
from jax.experimental.pallas import tpu as pltpu
from jax.sharding import PartitionSpec as P

ROUNDS = 2
SHARPNESS = 2.0
STEP_SIZE = 0.5
F32 = jnp.float32
BF16 = jnp.bfloat16
MESH = pl.DeviceIdType.MESH
LOADS = 8


def split3(x):
    high = x.astype(BF16)
    rest = x - high.astype(F32)
    mid = rest.astype(BF16)
    low = (rest - mid.astype(F32)).astype(BF16)
    return high, mid, low


def mm(a, b):
    return lax.dot_general(a, b, (((1,), (0,)), ((), ())), preferred_element_type=F32)


def mm_nt(a, b):
    return lax.dot_general(a, b, (((1,), (1,)), ((), ())), preferred_element_type=F32)


def iota(shape, dim):
    return lax.broadcasted_iota(jnp.int32, shape, dim)


def far_first(n):
    return sorted(range(1, n), key=lambda k: -min(k, n - k))


def vox_partners(nv, v):
    if nv == 16:
        x, z = v // 4, lax.rem(v, 4)
        hops = [(dx, dz) for dx in range(4) for dz in range(4) if dx or dz]
        hops.sort(key=lambda h: -(min(h[0], 4 - h[0]) + min(h[1], 4 - h[1])))
        return [lax.rem(x + dx, 4) * 4 + lax.rem(z + dz, 4) for dx, dz in hops]
    return [lax.rem(v + k, nv) for k in range(1, nv)]


def kernel(
    nv, ns, slots,
    map_ref, count_ref, target_ref, init_ref, dose_ref,
    out_ref, weights_ref,
    stage, fwd_w, bwd_w, left, right, got_left, got_right,
    col_hot, same3, col3, rep3, spare, target_slot, held_w, copies,
    whole, terms, parts, terms_both, parts_both, sums, lse_own, lse_twin, lse_parts,
    load_sem, vox_send, vox_recv, scen_send, scen_recv, lse_send, lse_recv,
):
    half = slots // 2
    beam_blocks = nv * 8
    v = lax.axis_index("vox")
    s_me = lax.axis_index("scen")
    ny = ns // 2
    y_me, core = s_me // 2, lax.rem(s_me, 2)
    own = pl.ds(pl.multiple_of(v * 8, 8), 8)
    vox_others = vox_partners(nv, v)
    twin = s_me + 1 - 2 * core
    chips = [lax.rem(y_me + k, ny) * 2 + c for k in far_first(ny) for c in range(2)]
    scen_others = chips + [twin]
    per_load = slots // LOADS

    def load(s, k):
        rows = pl.ds(k * per_load, per_load)
        return pltpu.make_async_copy(
            dose_ref.at[s, rows], stage.at[s, rows], load_sem.at[s, k]
        )

    for s in range(2):
        for k in range(LOADS):
            load(s, k).start()

    barrier = pltpu.get_barrier_semaphore()
    for t in vox_others:
        pl.semaphore_signal(barrier, inc=1, device_id={"vox": t}, device_id_type=MESH)
    for t in scen_others:
        pl.semaphore_signal(barrier, inc=1, device_id={"scen": t}, device_id_type=MESH)

    left[...] = jnp.zeros_like(left)
    right[...] = jnp.zeros_like(right)

    usable = (iota((128, slots), 1) < count_ref[0]).astype(F32)
    row_t = ((map_ref[0:1, :] == iota((128, slots), 0)).astype(F32) * usable).astype(BF16)
    col_t = (map_ref[1:2, :] == iota((beam_blocks, slots), 0)).astype(F32).astype(BF16)
    eye = (iota((slots, slots), 0) == iota((slots, slots), 1)).astype(F32).astype(BF16)
    eye3 = jnp.concatenate([eye] * 3, axis=0)
    row3_t = mm_nt(row_t, eye3).astype(BF16)
    row_hot = mm_nt(eye, row_t)
    row_b = row_hot.astype(BF16)
    col_hot[...] = mm_nt(eye, col_t).astype(BF16)
    same_all = mm(row_b, row3_t)
    same3[...] = same_all.astype(BF16)
    col3[...] = mm_nt(col_t, eye3).astype(BF16)
    place = iota((slots, 3 * slots), 1)
    earlier = jnp.sum(
        jnp.where(place < iota((slots, 3 * slots), 0), same_all, 0.0), axis=1, keepdims=True
    )
    rep_b = jnp.where(earlier < 0.5, row_hot, 0.0).astype(BF16)
    eye_row = (iota((128, 128), 0) == iota((128, 128), 1)).astype(F32).astype(BF16)
    picks = mm_nt(eye_row, jnp.concatenate([rep_b] * 3, axis=0))
    rep3[...] = picks.astype(BF16)
    covered = jnp.sum(picks, axis=1, keepdims=True)
    spare[...] = jnp.broadcast_to(jnp.where(covered > 0.5, 0.0, 1.0 / (2 * ns)), (128, 128))
    tgt = mm(row_b, jnp.concatenate(split3(target_ref[...]), axis=1))
    target_slot[...] = (tgt[:, 0:128] + tgt[:, 128:256]) + tgt[:, 256:384]

    pl.semaphore_wait(barrier, len(vox_others) + len(scen_others))

    def vox_copy(src, dst, slot, target):
        return pltpu.make_async_remote_copy(
            src_ref=src, dst_ref=dst, send_sem=vox_send.at[slot], recv_sem=vox_recv.at[slot],
            device_id={"vox": target}, device_id_type=MESH,
        )

    def vox_wait(slot, ref):
        rest = ref.at[pl.ds(0, (nv - 1) * 8)]
        pltpu.make_async_copy(rest, rest, vox_recv.at[slot]).wait()

    def gather_slot(r, s):
        return 2 + 2 * r + s

    def reduce_slot(r, s):
        return 6 + 3 * r + s

    whole[0, own, :] = init_ref[...]
    for t in vox_others:
        vox_copy(init_ref, whole.at[0, own], 0, t).start()

    def send_whole(slot, value):
        whole[slot, own, :] = value
        for t in vox_others:
            vox_copy(whole.at[slot, own], whole.at[slot, own], slot, t).start()

    def convert(s, k):
        load(s, k).wait()
        for u in range(per_load):
            n = k * per_load + u
            pair = lax.rem(n, half)
            at = pl.ds(pl.multiple_of((n // half) * 128, 128), 128)
            block = stage[s, n]
            high = block.astype(BF16)
            low = (block - high.astype(F32)).astype(BF16)
            bwd_w[s, pair, at, 0:128] = high
            bwd_w[s, pair, at, 128:256] = low
            fwd_w[s, pair, at, 0:128] = high.T
            fwd_w[s, pair, at, 128:256] = low.T

    for s in range(2):
        lax.fori_loop(0, LOADS, lambda k, c: (convert(s, k), c)[1], 0)

    def stack(k, pieces):
        for q, piece in enumerate(pieces):
            left[k, pl.ds(q, half, stride=8), :] = piece[0:half]
            right[k, pl.ds(q + 3, half, stride=8), :] = piece[half:slots]

    def multiply(k, outs, weights):
        for p in range(half):
            at = pl.ds(p * 8, 8)
            lhs = jnp.concatenate([left[k, at, :], right[k, at, :]], axis=1).astype(BF16)
            for out, s in outs:
                got = mm(lhs, weights[s, p])
                got_left[out, at, :] = got[:, 0:128]
                got_right[out, at, :] = got[:, 128:256]

    def collect(k):
        halves = []
        for base in (0, 3):
            total = None
            for q in (2, 1, 0):
                at = pl.ds(base + q, half, stride=8)
                term = got_left[k, at, :] + got_right[k, at, :]
                total = term if total is None else total + term
            halves.append(total)
        return jnp.concatenate(split3(jnp.concatenate(halves, axis=0)), axis=0)

    def pick(slot):
        picked = mm(col_hot[...], jnp.concatenate(split3(whole[slot]), axis=1))
        return [picked[:, 128 * q:128 * q + 128] for q in range(3)]

    def excess_of(k):
        return mm(same3[...], collect(k)) - target_slot[...]

    def push(k, weighted):
        stack(k, [piece.astype(F32) for piece in split3(weighted)])

    def descend(s, gradient):
        moved = jnp.maximum(copies[s] - STEP_SIZE * gradient, 0.0)
        copies[s] = moved
        return moved

    def add_up(terms_of):
        values = [terms_of(j) for j in range(nv)]
        while len(values) > 1:
            values = [a + b for a, b in zip(values[0::2], values[1::2])]
        return values[0]

    def merge(values):
        peak = functools.reduce(jnp.maximum, values)
        return peak + jnp.log(sum(jnp.exp(value - peak) for value in values))

    mine = pl.ds(pl.multiple_of(core * half, 8), half)

    def lse_copy(src, dst, r, k, target):
        return pltpu.make_async_remote_copy(
            src_ref=src, dst_ref=dst, send_sem=lse_send.at[r, k], recv_sem=lse_recv.at[r, k],
            device_id={"scen": target}, device_id_type=MESH,
        )

    def log_totals(r, scores):
        lse_own[r] = merge(scores)
        first = lse_copy(lse_own.at[r], lse_twin.at[r], r, 0, twin)
        first.start()
        first.wait_recv()
        lse_parts[r, y_me] = merge([lse_own[r], lse_twin[r]])
        for t in chips:
            spot = lse_parts.at[r, y_me, mine]
            lse_copy(spot, spot, r, 1, t).start()
        rest = lse_parts.at[r, pl.ds(0, ny - 1)]
        pltpu.make_async_copy(rest, rest, lse_recv.at[r, 1]).wait()
        return merge([lse_parts[r, j] for j in range(ny)])

    def scen_copy(r, t):
        return pltpu.make_async_remote_copy(
            src_ref=sums.at[r, s_me], dst_ref=sums.at[r, s_me],
            send_sem=scen_send.at[r], recv_sem=scen_recv.at[r],
            device_id={"scen": t}, device_id_type=MESH,
        )

    for s in range(2):
        copies[s] = init_ref[...]

    for r in range(ROUNDS):
        vox_wait(r, whole.at[r])
        stack(0, pick(r))
        multiply(0, [(0, 0), (1, 1)], fwd_w)
        excess = [excess_of(s) for s in range(2)]
        scores = [SHARPNESS * value * value for value in excess]
        totals = log_totals(r, scores)
        for s in range(2):
            held = jnp.exp(scores[s] - totals)
            held_w[s] = held
            push(2 + s, 2.0 * held * excess[s])
        for s in range(2):
            slot = reduce_slot(r, s)
            k = 2 * r + s
            multiply(2 + s, [(2 + s, s)], bwd_w)
            terms[k] = mm(col3[...], collect(2 + s))
            for t in vox_others:
                vox_copy(
                    terms.at[k, pl.ds(pl.multiple_of(t * 8, 8), 8)],
                    parts.at[k, own], slot, t,
                ).start()
            parts[k, own, :] = terms[k, own, :]
        if r == ROUNDS - 1:
            for s in range(2):
                pieces = jnp.concatenate(split3(held_w[s]), axis=0)
                weights_ref[pl.ds(s, 128, stride=2), :] = mm(rep3[...], pieces) + spare[...]
        for s in range(2):
            k = 2 * r + s
            vox_wait(reduce_slot(r, s), parts.at[k])
            gradient = add_up(lambda j: parts[k, 8 * j:8 * j + 8, :])
            send_whole(gather_slot(r, s), descend(s, gradient))

        slot = gather_slot(r, 0)
        vox_wait(slot, whole.at[slot])
        stack(0, pick(slot))
        multiply(0, [(0, 0)], fwd_w)
        slot = gather_slot(r, 1)
        vox_wait(slot, whole.at[slot])
        stack(1, pick(slot))
        push(2, 2.0 * held_w[0] * excess_of(0))
        multiply(1, [(1, 1)], fwd_w)
        multiply(2, [(2, 0)], bwd_w)
        push(3, 2.0 * held_w[1] * excess_of(1))
        terms_both[r, :, 0:8, :] = mm(col3[...], collect(2)).reshape(nv, 8, 128)
        multiply(3, [(3, 1)], bwd_w)
        terms_both[r, :, 8:16, :] = mm(col3[...], collect(3)).reshape(nv, 8, 128)
        slot = reduce_slot(r, 2)
        for t in vox_others:
            vox_copy(terms_both.at[r, t], parts_both.at[r, v], slot, t).start()
        parts_both[r, v] = terms_both[r, v]
        rest = parts_both.at[r, pl.ds(0, nv - 1)]
        pltpu.make_async_copy(rest, rest, vox_recv.at[slot]).wait()
        gradient = add_up(lambda j: parts_both[r, j])
        sums[r, s_me] = descend(0, gradient[0:8]) + descend(1, gradient[8:16])
        for t in scen_others:
            scen_copy(r, t).start()
        rest = sums.at[r, pl.ds(0, ns - 1)]
        pltpu.make_async_copy(rest, rest, scen_recv.at[r]).wait()
        total = sums[r, 0]
        for j in range(1, ns):
            total = total + sums[r, j]
        fluence = total / (2 * ns)
        if r < ROUNDS - 1:
            for s in range(2):
                copies[s] = fluence
            send_whole(r + 1, fluence)
        else:
            out_ref[...] = fluence

    for slot in range(6):
        rest = whole.at[0, pl.ds(0, (nv - 1) * 8)]
        pltpu.make_async_copy(rest, rest, vox_send.at[slot]).wait()
    for r in range(ROUNDS):
        for s in range(2):
            rest = whole.at[0, pl.ds(0, (nv - 1) * 8)]
            pltpu.make_async_copy(rest, rest, vox_send.at[reduce_slot(r, s)]).wait()
        rest = parts_both.at[r, pl.ds(0, nv - 1)]
        pltpu.make_async_copy(rest, rest, vox_send.at[reduce_slot(r, 2)]).wait()
        rest = sums.at[r, pl.ds(0, ns - 1)]
        pltpu.make_async_copy(rest, rest, scen_send.at[r]).wait()
        pltpu.make_async_copy(lse_own.at[r], lse_own.at[r], lse_send.at[r, 0]).wait()
        rest = lse_parts.at[r, pl.ds(0, ny - 1)]
        pltpu.make_async_copy(rest, rest, lse_send.at[r, 1]).wait()


def body(nv, ns, dose_blocks, block_map, block_counts, target, fluence_init):
    _, slots, side, _ = dose_blocks.shape
    half = slots // 2
    rows = target.shape[0] // side
    beam_blocks = nv * 8
    vmem = pl.BlockSpec(memory_space=pltpu.VMEM)
    out, weights = pl.pallas_call(
        functools.partial(kernel, nv, ns, slots),
        out_shape=(
            jax.ShapeDtypeStruct((8, side), F32),
            jax.ShapeDtypeStruct((2 * rows, side), F32),
        ),
        in_specs=[vmem, pl.BlockSpec(memory_space=pltpu.SMEM), vmem, vmem, pl.BlockSpec(memory_space=pl.ANY)],
        out_specs=(vmem, vmem),
        scratch_shapes=[
            pltpu.VMEM((2, slots, side, side), F32),
            pltpu.VMEM((2, half, 2 * side, 2 * side), BF16),
            pltpu.VMEM((2, half, 2 * side, 2 * side), BF16),
            pltpu.VMEM((4, 8 * half, side), F32),
            pltpu.VMEM((4, 8 * half, side), F32),
            pltpu.VMEM((4, 8 * half, side), F32),
            pltpu.VMEM((4, 8 * half, side), F32),
            pltpu.VMEM((slots, beam_blocks), BF16),
            pltpu.VMEM((slots, 3 * slots), BF16),
            pltpu.VMEM((beam_blocks, 3 * slots), BF16),
            pltpu.VMEM((rows, 3 * slots), BF16),
            pltpu.VMEM((rows, side), F32),
            pltpu.VMEM((slots, side), F32),
            pltpu.VMEM((2, slots, side), F32),
            pltpu.VMEM((2, 8, side), F32),
            pltpu.VMEM((6, beam_blocks, side), F32),
            pltpu.VMEM((4, beam_blocks, side), F32),
            pltpu.VMEM((4, beam_blocks, side), F32),
            pltpu.VMEM((ROUNDS, nv, 16, side), F32),
            pltpu.VMEM((ROUNDS, nv, 16, side), F32),
            pltpu.VMEM((ROUNDS, ns, 8, side), F32),
            pltpu.VMEM((ROUNDS, slots, side), F32),
            pltpu.VMEM((ROUNDS, slots, side), F32),
            pltpu.VMEM((ROUNDS, ns // 2, slots, side), F32),
            pltpu.SemaphoreType.DMA((2, LOADS)),
            pltpu.SemaphoreType.DMA((12,)),
            pltpu.SemaphoreType.DMA((12,)),
            pltpu.SemaphoreType.DMA((ROUNDS,)),
            pltpu.SemaphoreType.DMA((ROUNDS,)),
            pltpu.SemaphoreType.DMA((ROUNDS, 2)),
            pltpu.SemaphoreType.DMA((ROUNDS, 2)),
        ],
        compiler_params=pltpu.CompilerParams(
            collective_id=0, has_side_effects=True, vmem_limit_bytes=56 * 2**20
        ),
        name="robust_descent",
    )(
        block_map.T, block_counts, target.reshape(rows, side), fluence_init.reshape(8, side), dose_blocks
    )
    weights = weights.reshape(rows, 2, side).transpose(1, 0, 2)
    return out.reshape(-1), weights.reshape(2, -1)


def solution(mesh):
    nv, ns = mesh.shape["vox"], mesh.shape["scen"]
    placed = (P("scen", "vox", None, None), P("vox", None), P("vox"), P("vox"), P("vox"))
    return jax.shard_map(
        functools.partial(body, nv, ns),
        mesh=mesh, in_specs=placed, out_specs=(P("vox"), P("scen", "vox")), check_vma=False,
    )
```

time: 86.7 us -> 81.3 us (0.938)
  Pallas kernels: 80.9 us -> 77 us
  local copies, waits for them, and re-layouts: 4.33 us -> 2.85 us
    pallas_call x1, Pallas kernels: 80.9 us -> 77 us  [body(): pl.pallas_call(functools.partial(kernel, nv, ns, slots), out_shape=(jax.S...]
    unnamed x3 -> x2, local copies, waits for them, and re-layouts: 4.33 us -> 2.85 us
where the time goes in v2:
time: 81.3 us; the launch traced here: 81.1 us
  Pallas kernels  77 us (95%)
  local copies, waits for them, and re-layouts  2.85 us (4%)
  between operations  1.28 us (2%)
    pallas_call x1, Pallas kernels, body(): pl.pallas_call(functools.partial(kernel, nv, ns, slots), out_shape=(jax.S...  77 us
    unnamed x2, local copies, waits for them, and re-layouts  2.85 us

profile of v2, /device:TPU:1, one launch (start us, length us, event | category | flops | bytes accessed | tf_op | source)
XLA Modules:
  0.0 81.1 jit_solution(13970769496948766527)
XLA Ops:
  1.3 77.0 %robust_descent.1 = (f32[8,128]{1,0:T(8,128)}, f32[256,128]{1,0:T(8,128)}) custom-call(s32[2,80]{1,0:T(2,128)} %bitcast.13, s32[1]{0:T(128)S(6)} %copy.10.count_ref, f32[128,128]{1,0:T(8,128)} %bitcast.10, f32[8,128]{1,0:T(8,128)} %bitcast.11, f32[2,80,128,128]{3,2,1,0:T(8,128)} %dose_ref.1), custom_call_target="tpu_custom_call" | custom-call | tf_op jit(solution)/shard_map/robust_descent/pallas_call | solution.py:334
  78.3 1.3 %copy.11 = f32[1024]{0:T(1024)} copy(f32[1024]{0:T(1024)} %bitcast.12) | data formatting | bytes 8192
  79.5 1.6 %copy.12 = f32[2,16384]{1,0:T(2,128)} copy(f32[2,16384]{1,0:T(2,128)} %bitcast.9) | data formatting | bytes 262144

commit v3 on v2

--- a/solution.py
+++ b/solution.py
@@ -51,12 +51,12 @@
 
 def kernel(
     nv, ns, slots,
-    map_ref, count_ref, target_ref, init_ref, dose_ref,
+    map_hbm, count_hbm, target_hbm, init_hbm, dose_ref,
     out_ref, weights_ref,
     stage, fwd_w, bwd_w, left, right, got_left, got_right,
     col_hot, same3, col3, rep3, spare, target_slot, held_w, copies,
     whole, terms, parts, terms_both, parts_both, sums, lse_own, lse_twin, lse_parts,
-    load_sem, vox_send, vox_recv, scen_send, scen_recv, lse_send, lse_recv,
+    map_ref, count_ref, target_ref, init_ref, small_sem, load_sem, vox_send, vox_recv, scen_send, scen_recv, lse_send, lse_recv,
 ):
     half = slots // 2
     beam_blocks = nv * 8
@@ -77,18 +77,28 @@
             dose_ref.at[s, rows], stage.at[s, rows], load_sem.at[s, k]
         )
 
-    for s in range(2):
-        for k in range(LOADS):
-            load(s, k).start()
-
     barrier = pltpu.get_barrier_semaphore()
     for t in vox_others:
         pl.semaphore_signal(barrier, inc=1, device_id={"vox": t}, device_id_type=MESH)
     for t in scen_others:
         pl.semaphore_signal(barrier, inc=1, device_id={"scen": t}, device_id_type=MESH)
 
+    small = [
+        pltpu.make_async_copy(src, dst, small_sem.at[k])
+        for k, (src, dst) in enumerate((
+            (map_hbm, map_ref), (count_hbm, count_ref), (init_hbm, init_ref), (target_hbm, target_ref)
+        ))
+    ]
+    for copy in small:
+        copy.start()
     left[...] = jnp.zeros_like(left)
     right[...] = jnp.zeros_like(right)
+
+    for copy in small:
+        copy.wait()
+    for s in range(2):
+        for k in range(LOADS):
+            load(s, k).start()
 
     usable = (iota((128, slots), 1) < count_ref[0]).astype(F32)
     row_t = ((map_ref[0:1, :] == iota((128, slots), 0)).astype(F32) * usable).astype(BF16)
@@ -325,6 +335,11 @@
         pltpu.make_async_copy(rest, rest, lse_send.at[r, 1]).wait()
 
 
+def hand_on(fluence_ref, weights_ref, fluence_out, weights_out):
+    fluence_out[...] = fluence_ref[...]
+    weights_out[...] = weights_ref[...]
+
+
 def body(nv, ns, dose_blocks, block_map, block_counts, target, fluence_init):
     _, slots, side, _ = dose_blocks.shape
     half = slots // 2
@@ -337,7 +352,7 @@
             jax.ShapeDtypeStruct((8, side), F32),
             jax.ShapeDtypeStruct((2 * rows, side), F32),
         ),
-        in_specs=[vmem, pl.BlockSpec(memory_space=pltpu.SMEM), vmem, vmem, pl.BlockSpec(memory_space=pl.ANY)],
+        in_specs=[pl.BlockSpec(memory_space=pltpu.HBM)] * 5,
         out_specs=(vmem, vmem),
         scratch_shapes=[
             pltpu.VMEM((2, slots, side, side), F32),
@@ -364,6 +379,11 @@
             pltpu.VMEM((ROUNDS, slots, side), F32),
             pltpu.VMEM((ROUNDS, slots, side), F32),
             pltpu.VMEM((ROUNDS, ns // 2, slots, side), F32),
+            pltpu.VMEM((2, slots), jnp.int32),
+            pltpu.SMEM((1,), jnp.int32),
+            pltpu.VMEM((rows, side), F32),
+            pltpu.VMEM((8, side), F32),
+            pltpu.SemaphoreType.DMA((4,)),
             pltpu.SemaphoreType.DMA((2, LOADS)),
             pltpu.SemaphoreType.DMA((12,)),
             pltpu.SemaphoreType.DMA((12,)),
@@ -373,12 +393,23 @@
             pltpu.SemaphoreType.DMA((ROUNDS, 2)),
         ],
         compiler_params=pltpu.CompilerParams(
-            collective_id=0, has_side_effects=True, vmem_limit_bytes=56 * 2**20
+            collective_id=0, has_side_effects=True, vmem_limit_bytes=52 * 2**20
         ),
         name="robust_descent",
     )(
-        block_map.T, block_counts, target.reshape(rows, side), fluence_init.reshape(8, side), dose_blocks
+        pltpu.with_memory_space_constraint(block_map.T, pltpu.HBM), block_counts, pltpu.with_memory_space_constraint(target.reshape(rows, side), pltpu.HBM), pltpu.with_memory_space_constraint(fluence_init.reshape(8, side), pltpu.HBM), dose_blocks
     )
+    out, weights = pl.pallas_call(
+        hand_on,
+        out_shape=(
+            jax.ShapeDtypeStruct((8, side), F32),
+            jax.ShapeDtypeStruct((2 * rows, side), F32),
+        ),
+        in_specs=[vmem, vmem],
+        out_specs=(vmem, vmem),
+        compiler_params=pltpu.CompilerParams(vmem_limit_bytes=2**20),
+        name="hand_on",
+    )(out, weights)
     weights = weights.reshape(rows, 2, side).transpose(1, 0, 2)
     return out.reshape(-1), weights.reshape(2, -1)
 

time: 81.3 us -> 77.7 us (0.956)
  local copies, waits for them, and re-layouts: 2.85 us -> 0 us
    unnamed x2 -> x0, local copies, waits for them, and re-layouts: 2.85 us -> none
    pallas_call x1, Pallas kernels: 77 us -> 75.6 us  [body(): pl.pallas_call(functools.partial(kernel, nv, ns, slots), out_shape=(jax.S...]
where the time goes in v3:
time: 77.7 us; the launch traced here: 77.5 us
  Pallas kernels  76.2 us (98%)
  between operations  1.28 us (2%)
    pallas_call x1, Pallas kernels, body(): pl.pallas_call(functools.partial(kernel, nv, ns, slots), out_shape=(jax.S...  75.6 us

profile of v3, /device:TPU:1, one launch (start us, length us, event | category | flops | bytes accessed | tf_op | source)
XLA Modules:
  0.0 77.5 jit_solution(16845712547542399746)
XLA Ops:
  1.3 75.6 %robust_descent.1 = (f32[8,128]{1,0:T(8,128)S(1)}, f32[256,128]{1,0:T(8,128)S(1)}) custom-call(s32[2,80]{1,0:T(2,128)} %bitcast.11, s32[1]{0:T(128)S(6)} %copy.8.count_hbm, f32[128,128]{1,0:T(8,128)} %bitcast.9, f32[8,128]{1,0:T(8,128)} %bitcast.10, f32[2,80,128,128]{3,2,1,0:T(8,128)} %dose_ref.1), custom_call_target="tpu_custom_call" | custom-call | tf_op jit(solution)/shard_map/robust_descent/pallas_call | solution.py:349
  76.8 0.7 hand_on.1

commit v4 on v3

--- a/solution.py
+++ b/solution.py
@@ -13,7 +13,8 @@
 F32 = jnp.float32
 BF16 = jnp.bfloat16
 MESH = pl.DeviceIdType.MESH
-LOADS = 8
+LOADS = 5
+VECTOR_SLOTS = 16
 
 
 def split3(x):
@@ -55,10 +56,11 @@
     out_ref, weights_ref,
     stage, fwd_w, bwd_w, left, right, got_left, got_right,
     col_hot, same3, col3, rep3, spare, target_slot, held_w, copies,
-    whole, terms, parts, terms_both, parts_both, sums, lse_own, lse_twin, lse_parts,
+    row_in, row_out, whole, terms, parts, terms_both, parts_both, sums, lse_own, lse_twin, lse_parts,
     map_ref, count_ref, target_ref, init_ref, small_sem, load_sem, vox_send, vox_recv, scen_send, scen_recv, lse_send, lse_recv,
 ):
     half = slots // 2
+    pairs = (slots - VECTOR_SLOTS) // 2
     beam_blocks = nv * 8
     v = lax.axis_index("vox")
     s_me = lax.axis_index("scen")
@@ -156,8 +158,8 @@
         load(s, k).wait()
         for u in range(per_load):
             n = k * per_load + u
-            pair = lax.rem(n, half)
-            at = pl.ds(pl.multiple_of((n // half) * 128, 128), 128)
+            pair = lax.rem(n, pairs)
+            at = pl.ds(pl.multiple_of((n // pairs) * 128, 128), 128)
             block = stage[s, n]
             high = block.astype(BF16)
             low = (block - high.astype(F32)).astype(BF16)
@@ -167,42 +169,78 @@
             fwd_w[s, pair, at, 128:256] = low.T
 
     for s in range(2):
-        lax.fori_loop(0, LOADS, lambda k, c: (convert(s, k), c)[1], 0)
+        lax.fori_loop(0, 2 * pairs // per_load, lambda k, c: (convert(s, k), c)[1], 0)
+        for k in range(2 * pairs // per_load, LOADS):
+            load(s, k).wait()
 
     def stack(k, pieces):
         for q, piece in enumerate(pieces):
-            left[k, pl.ds(q, half, stride=8), :] = piece[0:half]
-            right[k, pl.ds(q + 3, half, stride=8), :] = piece[half:slots]
-
-    def multiply(k, outs, weights):
-        for p in range(half):
-            at = pl.ds(p * 8, 8)
-            lhs = jnp.concatenate([left[k, at, :], right[k, at, :]], axis=1).astype(BF16)
-            for out, s in outs:
-                got = mm(lhs, weights[s, p])
-                got_left[out, at, :] = got[:, 0:128]
-                got_right[out, at, :] = got[:, 128:256]
+            left[k, pl.ds(q, pairs, stride=8), :] = piece[0:pairs]
+            right[k, pl.ds(q + 3, pairs, stride=8), :] = piece[pairs:2 * pairs]
+
+    def tile(k, out, s, p, weights):
+        at = pl.ds(p * 8, 8)
+        lhs = jnp.concatenate([left[k, at, :], right[k, at, :]], axis=1).astype(BF16)
+        got = mm(lhs, weights[s, p])
+        got_left[out, at, :] = got[:, 0:128]
+        got_right[out, at, :] = got[:, 128:256]
+
+    lane = iota((128, 128), 1)
+
+    def multiply_forward(k, outs):
+        tiles = [(out, s, p) for out, s in outs for p in range(pairs)]
+        rows = [(out, s, n) for out, s in outs for n in range(VECTOR_SLOTS)]
+        done = 0
+        sums_t = {out: jnp.zeros((128, 128), F32) for out, s in outs}
+        for m, (out, s, p) in enumerate(tiles):
+            tile(k, out, s, p, fwd_w)
+            while done * len(tiles) < (m + 1) * len(rows):
+                out, s, n = rows[done]
+                done += 1
+                product = stage[s, 2 * pairs + n] * row_in[k, n:n + 1, :]
+                dose = jnp.sum(product, axis=1, keepdims=True)
+                sums_t[out] = jnp.where(lane == n, dose, sums_t[out])
+                if n == VECTOR_SLOTS - 1:
+                    row_out[out] = sums_t[out].T[0:VECTOR_SLOTS]
+
+    def multiply_backward(k, s, column):
+        n = 0
+        for p in range(pairs):
+            tile(k, k, s, p, bwd_w)
+            while n * pairs < (p + 1) * VECTOR_SLOTS:
+                product = stage[s, 2 * pairs + n] * column[:, n:n + 1]
+                row_out[k, n:n + 1, :] = jnp.sum(product, axis=0, keepdims=True)
+                n += 1
 
     def collect(k):
-        halves = []
+        blocks = []
         for base in (0, 3):
             total = None
             for q in (2, 1, 0):
-                at = pl.ds(base + q, half, stride=8)
+                at = pl.ds(base + q, pairs, stride=8)
                 term = got_left[k, at, :] + got_right[k, at, :]
                 total = term if total is None else total + term
-            halves.append(total)
-        return jnp.concatenate(split3(jnp.concatenate(halves, axis=0)), axis=0)
+            blocks.append(total)
+        blocks.append(row_out[k])
+        return jnp.concatenate(split3(jnp.concatenate(blocks, axis=0)), axis=0)
 
     def pick(slot):
         picked = mm(col_hot[...], jnp.concatenate(split3(whole[slot]), axis=1))
         return [picked[:, 128 * q:128 * q + 128] for q in range(3)]
 
+    def load_forward(k, pieces):
+        stack(k, pieces)
+        high, mid, low = (piece[2 * pairs:] for piece in pieces)
+        row_in[k] = high + (mid + low)
+
     def excess_of(k):
         return mm(same3[...], collect(k)) - target_slot[...]
 
-    def push(k, weighted):
+    def load_backward(k, weighted):
         stack(k, [piece.astype(F32) for piece in split3(weighted)])
+        rest = weighted[2 * pairs:]
+        fill = jnp.zeros((128 - VECTOR_SLOTS, 128), F32)
+        return jnp.concatenate([rest, fill], axis=0).T
 
     def descend(s, gradient):
         moved = jnp.maximum(copies[s] - STEP_SIZE * gradient, 0.0)
@@ -252,19 +290,20 @@
 
     for r in range(ROUNDS):
         vox_wait(r, whole.at[r])
-        stack(0, pick(r))
-        multiply(0, [(0, 0), (1, 1)], fwd_w)
+        load_forward(0, pick(r))
+        multiply_forward(0, [(0, 0), (1, 1)])
         excess = [excess_of(s) for s in range(2)]
         scores = [SHARPNESS * value * value for value in excess]
         totals = log_totals(r, scores)
+        columns = []
         for s in range(2):
             held = jnp.exp(scores[s] - totals)
             held_w[s] = held
-            push(2 + s, 2.0 * held * excess[s])
+            columns.append(load_backward(2 + s, 2.0 * held * excess[s]))
         for s in range(2):
             slot = reduce_slot(r, s)
             k = 2 * r + s
-            multiply(2 + s, [(2 + s, s)], bwd_w)
+            multiply_backward(2 + s, s, columns[s])
             terms[k] = mm(col3[...], collect(2 + s))
             for t in vox_others:
                 vox_copy(
@@ -284,17 +323,17 @@
 
         slot = gather_slot(r, 0)
         vox_wait(slot, whole.at[slot])
-        stack(0, pick(slot))
-        multiply(0, [(0, 0)], fwd_w)
+        load_forward(0, pick(slot))
+        multiply_forward(0, [(0, 0)])
         slot = gather_slot(r, 1)
         vox_wait(slot, whole.at[slot])
-        stack(1, pick(slot))
-        push(2, 2.0 * held_w[0] * excess_of(0))
-        multiply(1, [(1, 1)], fwd_w)
-        multiply(2, [(2, 0)], bwd_w)
-        push(3, 2.0 * held_w[1] * excess_of(1))
+        load_forward(1, pick(slot))
+        column = load_backward(2, 2.0 * held_w[0] * excess_of(0))
+        multiply_forward(1, [(1, 1)])
+        multiply_backward(2, 0, column)
+        column = load_backward(3, 2.0 * held_w[1] * excess_of(1))
         terms_both[r, :, 0:8, :] = mm(col3[...], collect(2)).reshape(nv, 8, 128)
-        multiply(3, [(3, 1)], bwd_w)
+        multiply_backward(3, 1, column)
         terms_both[r, :, 8:16, :] = mm(col3[...], collect(3)).reshape(nv, 8, 128)
         slot = reduce_slot(r, 2)
         for t in vox_others:
@@ -342,7 +381,7 @@
 
 def body(nv, ns, dose_blocks, block_map, block_counts, target, fluence_init):
     _, slots, side, _ = dose_blocks.shape
-    half = slots // 2
+    pairs = (slots - VECTOR_SLOTS) // 2
     rows = target.shape[0] // side
     beam_blocks = nv * 8
     vmem = pl.BlockSpec(memory_space=pltpu.VMEM)
@@ -356,12 +395,12 @@
         out_specs=(vmem, vmem),
         scratch_shapes=[
             pltpu.VMEM((2, slots, side, side), F32),
-            pltpu.VMEM((2, half, 2 * side, 2 * side), BF16),
-            pltpu.VMEM((2, half, 2 * side, 2 * side), BF16),
-            pltpu.VMEM((4, 8 * half, side), F32),
-            pltpu.VMEM((4, 8 * half, side), F32),
-            pltpu.VMEM((4, 8 * half, side), F32),
-            pltpu.VMEM((4, 8 * half, side), F32),
+            pltpu.VMEM((2, pairs, 2 * side, 2 * side), BF16),
+            pltpu.VMEM((2, pairs, 2 * side, 2 * side), BF16),
+            pltpu.VMEM((4, 8 * pairs, side), F32),
+            pltpu.VMEM((4, 8 * pairs, side), F32),
+            pltpu.VMEM((4, 8 * pairs, side), F32),
+            pltpu.VMEM((4, 8 * pairs, side), F32),
             pltpu.VMEM((slots, beam_blocks), BF16),
             pltpu.VMEM((slots, 3 * slots), BF16),
             pltpu.VMEM((beam_blocks, 3 * slots), BF16),
@@ -370,6 +409,8 @@
             pltpu.VMEM((slots, side), F32),
             pltpu.VMEM((2, slots, side), F32),
             pltpu.VMEM((2, 8, side), F32),
+            pltpu.VMEM((4, VECTOR_SLOTS, side), F32),
+            pltpu.VMEM((4, VECTOR_SLOTS, side), F32),
             pltpu.VMEM((6, beam_blocks, side), F32),
             pltpu.VMEM((4, beam_blocks, side), F32),
             pltpu.VMEM((4, beam_blocks, side), F32),

time: 77.7 us -> 76.1 us (0.979)
  Pallas kernels: 76.2 us -> 74.6 us
    pallas_call x1, Pallas kernels: 75.6 us -> 74 us  [body(): pl.pallas_call(functools.partial(kernel, nv, ns, slots), out_shape=(jax.S...]
where the time goes in v4:
time: 76.1 us; the launch traced here: 75.9 us
  Pallas kernels  74.6 us (98%)
  between operations  1.28 us (2%)
    pallas_call x1, Pallas kernels, body(): pl.pallas_call(functools.partial(kernel, nv, ns, slots), out_shape=(jax.S...  74 us

profile of v4, /device:TPU:1, one launch (start us, length us, event | category | flops | bytes accessed | tf_op | source)
XLA Modules:
  0.0 75.9 jit_solution(15294612627095880788)
XLA Ops:
  1.3 74.0 %robust_descent.1 = (f32[8,128]{1,0:T(8,128)S(1)}, f32[256,128]{1,0:T(8,128)S(1)}) custom-call(s32[2,80]{1,0:T(2,128)} %bitcast.11, s32[1]{0:T(128)S(6)} %copy.8.count_hbm, f32[128,128]{1,0:T(8,128)} %bitcast.9, f32[8,128]{1,0:T(8,128)} %bitcast.10, f32[2,80,128,128]{3,2,1,0:T(8,128)} %dose_ref.1), custom_call_target="tpu_custom_call" | custom-call | tf_op jit(solution)/shard_map/robust_descent/pallas_call | solution.py:388
  75.2 0.7 hand_on.1

commit v5 on v4

--- a/solution.py
+++ b/solution.py
@@ -13,8 +13,9 @@
 F32 = jnp.float32
 BF16 = jnp.bfloat16
 MESH = pl.DeviceIdType.MESH
-LOADS = 5
-VECTOR_SLOTS = 16
+LOADS = 4
+VECTOR_SLOTS = 24
+GROUP = 4
 
 
 def split3(x):
@@ -154,13 +155,11 @@
         for t in vox_others:
             vox_copy(whole.at[slot, own], whole.at[slot, own], slot, t).start()
 
-    def convert(s, k):
-        load(s, k).wait()
-        for u in range(per_load):
-            n = k * per_load + u
-            pair = lax.rem(n, pairs)
-            at = pl.ds(pl.multiple_of((n // pairs) * 128, 128), 128)
-            block = stage[s, n]
+    def convert(s, n):
+        for u in range(GROUP):
+            pair = lax.rem(n + u, half)
+            at = pl.ds(pl.multiple_of(((n + u) // half) * 128, 128), 128)
+            block = stage[s, n + u]
             high = block.astype(BF16)
             low = (block - high.astype(F32)).astype(BF16)
             bwd_w[s, pair, at, 0:128] = high
@@ -169,14 +168,21 @@
             fwd_w[s, pair, at, 128:256] = low.T
 
     for s in range(2):
-        lax.fori_loop(0, 2 * pairs // per_load, lambda k, c: (convert(s, k), c)[1], 0)
-        for k in range(2 * pairs // per_load, LOADS):
+        for k in range(LOADS):
             load(s, k).wait()
+            begin = k * per_load
+            end = min(begin + per_load, begin // half * half + pairs)
+            lax.fori_loop(
+                0, (end - begin) // GROUP,
+                lambda g, c: (convert(s, begin + g * GROUP), c)[1], 0,
+            )
+
+    others = [n for n in range(slots) if n % half >= pairs]
 
     def stack(k, pieces):
         for q, piece in enumerate(pieces):
             left[k, pl.ds(q, pairs, stride=8), :] = piece[0:pairs]
-            right[k, pl.ds(q + 3, pairs, stride=8), :] = piece[pairs:2 * pairs]
+            right[k, pl.ds(q + 3, pairs, stride=8), :] = piece[half:half + pairs]
 
     def tile(k, out, s, p, weights):
         at = pl.ds(p * 8, 8)
@@ -189,7 +195,7 @@
 
     def multiply_forward(k, outs):
         tiles = [(out, s, p) for out, s in outs for p in range(pairs)]
-        rows = [(out, s, n) for out, s in outs for n in range(VECTOR_SLOTS)]
+        rows = [(out, s, n) for out, s in outs for n in others]
         done = 0
         sums_t = {out: jnp.zeros((128, 128), F32) for out, s in outs}
         for m, (out, s, p) in enumerate(tiles):
@@ -197,32 +203,34 @@
             while done * len(tiles) < (m + 1) * len(rows):
                 out, s, n = rows[done]
                 done += 1
-                product = stage[s, 2 * pairs + n] * row_in[k, n:n + 1, :]
+                product = stage[s, n] * row_in[k, n:n + 1, :]
                 dose = jnp.sum(product, axis=1, keepdims=True)
                 sums_t[out] = jnp.where(lane == n, dose, sums_t[out])
-                if n == VECTOR_SLOTS - 1:
-                    row_out[out] = sums_t[out].T[0:VECTOR_SLOTS]
+                if n == others[-1]:
+                    by_row = sums_t[out].T
+                    for base in (0, half):
+                        span = slice(base + pairs, base + half)
+                        row_out[out, span, :] = by_row[span]
 
     def multiply_backward(k, s, column):
-        n = 0
+        done = 0
         for p in range(pairs):
             tile(k, k, s, p, bwd_w)
-            while n * pairs < (p + 1) * VECTOR_SLOTS:
-                product = stage[s, 2 * pairs + n] * column[:, n:n + 1]
+            while done * pairs < (p + 1) * len(others):
+                n = others[done]
+                done += 1
+                product = stage[s, n] * column[:, n:n + 1]
                 row_out[k, n:n + 1, :] = jnp.sum(product, axis=0, keepdims=True)
-                n += 1
 
     def collect(k):
-        blocks = []
-        for base in (0, 3):
+        for row, base in ((0, 0), (half, 3)):
             total = None
             for q in (2, 1, 0):
                 at = pl.ds(base + q, pairs, stride=8)
                 term = got_left[k, at, :] + got_right[k, at, :]
                 total = term if total is None else total + term
-            blocks.append(total)
-        blocks.append(row_out[k])
-        return jnp.concatenate(split3(jnp.concatenate(blocks, axis=0)), axis=0)
+            row_out[k, row:row + pairs, :] = total
+        return jnp.concatenate(split3(row_out[k]), axis=0)
 
     def pick(slot):
         picked = mm(col_hot[...], jnp.concatenate(split3(whole[slot]), axis=1))
@@ -230,7 +238,7 @@
 
     def load_forward(k, pieces):
         stack(k, pieces)
-        high, mid, low = (piece[2 * pairs:] for piece in pieces)
+        high, mid, low = pieces
         row_in[k] = high + (mid + low)
 
     def excess_of(k):
@@ -238,9 +246,8 @@
 
     def load_backward(k, weighted):
         stack(k, [piece.astype(F32) for piece in split3(weighted)])
-        rest = weighted[2 * pairs:]
-        fill = jnp.zeros((128 - VECTOR_SLOTS, 128), F32)
-        return jnp.concatenate([rest, fill], axis=0).T
+        fill = jnp.zeros((128 - slots, 128), F32)
+        return jnp.concatenate([weighted, fill], axis=0).T
 
     def descend(s, gradient):
         moved = jnp.maximum(copies[s] - STEP_SIZE * gradient, 0.0)
@@ -409,8 +416,8 @@
             pltpu.VMEM((slots, side), F32),
             pltpu.VMEM((2, slots, side), F32),
             pltpu.VMEM((2, 8, side), F32),
-            pltpu.VMEM((4, VECTOR_SLOTS, side), F32),
-            pltpu.VMEM((4, VECTOR_SLOTS, side), F32),
+            pltpu.VMEM((4, slots, side), F32),
+            pltpu.VMEM((4, slots, side), F32),
             pltpu.VMEM((6, beam_blocks, side), F32),
             pltpu.VMEM((4, beam_blocks, side), F32),
             pltpu.VMEM((4, beam_blocks, side), F32),

time: 76.1 us -> 75.7 us (level)
  no operation moved by 1% of the time
where the time goes in v5:
time: 75.7 us; the launch traced here: 75.6 us
  Pallas kernels  74.3 us (98%)
  between operations  1.28 us (2%)
    pallas_call x1, Pallas kernels, body(): pl.pallas_call(functools.partial(kernel, nv, ns, slots), out_shape=(jax.S...  73.6 us

profile of v5, /device:TPU:1, one launch (start us, length us, event | category | flops | bytes accessed | tf_op | source)
XLA Modules:
  0.0 75.6 jit_solution(15591764572464239084)
XLA Ops:
  1.3 73.6 %robust_descent.1 = (f32[8,128]{1,0:T(8,128)S(1)}, f32[256,128]{1,0:T(8,128)S(1)}) custom-call(s32[2,80]{1,0:T(2,128)} %bitcast.11, s32[1]{0:T(128)S(6)} %copy.8.count_hbm, f32[128,128]{1,0:T(8,128)} %bitcast.9, f32[8,128]{1,0:T(8,128)} %bitcast.10, f32[2,80,128,128]{3,2,1,0:T(8,128)} %dose_ref.1), custom_call_target="tpu_custom_call" | custom-call | tf_op jit(solution)/shard_map/robust_descent/pallas_call | solution.py:395
  74.9 0.7 hand_on.1
